TPU v7x, 256 devices: a whole 4x4x8 slice. The times are simulated.
256 devices in a mesh: seg: 64 (over x, z, core), pitch: 4 (over y).
Axes of the slice: x: 4, y: 4, z: 8, core: 2. Of those that a mesh axis runs over, the one named last changes fastest.
Arguments:
- state: float32 [1024, 8, 5, 49, 128], P('seg', 'pitch'), may hold values from -6 to 6
- advect: float32 [1024, 8, 5, 128], P('seg', 'pitch'), may hold values from 0.2 to 1
- viscous: float32 [1024, 8, 5, 128], P('seg', 'pitch'), may hold values from 0.1 to 0.5
- inverse: bfloat16 [1024, 8, 5, 5, 128], P('seg', 'pitch'), as said below
- lower: float32 [1024, 8, 5, 5, 128], P('seg', 'pitch'), as said below
- upper: float32 [1024, 8, 5, 5, 128], P('seg', 'pitch'), as said below
- blades: int32 [2], replicated, may hold values from 20 to 90
- harmonic: int32 [24], replicated, may hold values from 1 to 8, as said below
Outputs:
- update: float32 [1024, 8, 5, 49, 128], P('seg', 'pitch')
Inputs may be any that keep to these rules, and one draw needn't show every extreme that they name: inverse holds each cell's given block inverse. lower holds each cell's upstream coupling, already multiplied by the block inverse and negated. upper holds each cell's downstream coupling, already multiplied by the block inverse and negated. `harmonic`: the mode multiples are not all equal.
All inputs are finite; a program needn't handle non-finite values.
Results may differ from a plain program's by a relative error of at most 0.0003.
Values sent between devices are 32-bit elements; how exact they have to be, the bound alone decides.
A program may use at most 128 MiB of HBM per device.

v0:
```python
import math

import jax
import jax.numpy as jnp
from jax import lax
from jax.sharding import PartitionSpec as P


def prefix_2(part, axis, combine, identity, reverse):
    count = lax.axis_size(axis)
    place = lax.axis_index(axis)
    ahead = count - 1 - place if reverse else place
    gathered = jax.tree.map(lambda a: lax.all_gather(a, axis), part)
    state = jax.tree.map(lambda a, e: jnp.zeros_like(a) + jnp.asarray(e, a.dtype), part, identity)

    def one(turn, state):
        source = count - 1 - turn if reverse else turn
        return combine(
            state, jax.tree.map(lambda a: lax.dynamic_index_in_dim(a, source, 0, False), gathered)
        )

    return lax.fori_loop(0, ahead, one, state)


def with_halo(cells, sides, width, closed):
    for axis, dim in sides:
        count = lax.axis_size(axis)
        ends = count if closed else count - 1
        head = lax.slice_in_dim(cells, 0, width, axis=dim)
        tail = lax.slice_in_dim(cells, cells.shape[dim] - width, cells.shape[dim], axis=dim)
        cells = jnp.concatenate(
            [
                lax.ppermute(tail, axis, [(i, (i + 1) % count) for i in range(ends)]),
                cells,
                lax.ppermute(head, axis, [((i + 1) % count, i) for i in range(ends)]),
            ],
            axis=dim,
        )
    return cells


def spectral_tables(blades, harmonic, fourier_components):
    sampled_moments = 2 * fourier_components + 1
    moment_number = jnp.arange(sampled_moments, dtype=jnp.int32)
    blade_spacing_displacement = moment_number[:, None] - moment_number[None, :]
    cyclic_folded = jnp.mod(blade_spacing_displacement, sampled_moments)
    parity = 1.0 - 2.0 * jnp.mod(blade_spacing_displacement, 2).astype(jnp.float32)
    protected_sinus = jnp.where(
        blade_spacing_displacement == 0,
        jnp.float32(1.0),
        jnp.sin(math.pi * blade_spacing_displacement.astype(jnp.float32) / sampled_moments),
    )
    derive = jnp.where(
        blade_spacing_displacement == 0, jnp.float32(0.0), 0.5 * parity / protected_sinus
    )
    rotor_blades = blades[0].astype(jnp.float32)
    stator = blades[1].astype(jnp.float32)
    blade_ratio = stator / rotor_blades
    frequency = blade_ratio / fourier_components
    fourier_wavenumbers = jnp.arange(1, fourier_components + 1, dtype=jnp.int32)
    lag_amounts = 2.0 * math.pi * harmonic.astype(jnp.float32) * blade_ratio
    lag_radians = jnp.mod(
        fourier_wavenumbers[:, None, None] * cyclic_folded[None], sampled_moments
    ).astype(jnp.float32) * (2.0 * math.pi / sampled_moments)
    forward_lag_angle = (
        1.0 + 2.0 * jnp.sum(jnp.cos(lag_radians + lag_amounts[:, None, None]), axis=0)
    ) / sampled_moments
    rearward_displacement = (
        1.0 + 2.0 * jnp.sum(jnp.cos(lag_radians - lag_amounts[:, None, None]), axis=0)
    ) / sampled_moments
    return (derive, frequency, forward_lag_angle, rearward_displacement)


def apply_block(left, right):
    return jnp.sum(left[..., :, :, None, :] * right[..., None, :, :, :], axis=-3)


def combine(earlier, later):
    return (apply_block(later[0], earlier[0]), apply_block(later[0], earlier[1]) + later[1])


def incoming(product, outflow, from_right):
    identity = jnp.broadcast_to(
        jnp.eye(product.shape[1], dtype=jnp.float32)[None, :, :, None], product.shape
    )
    prefix = prefix_2(
        (product, outflow), "seg", combine, (identity, jnp.zeros_like(outflow)), from_right
    )
    return prefix[1]


def sweep_step(current_pair, pieces):
    current, product = current_pair
    source_cell, coupling_cell = pieces
    current = source_cell + apply_block(coupling_cell, current)
    return ((current, apply_block(coupling_cell, product)), None)


def sweep_fill(current, pieces):
    source_cell, coupling_cell = pieces
    current = source_cell + apply_block(coupling_cell, current)
    return (current, current)


def line_sweep(sources, couplings, from_right):
    components = sources.shape[2]
    initial = jnp.zeros_like(sources[0])
    identity = jnp.broadcast_to(
        jnp.eye(components, dtype=jnp.float32)[None, :, :, None], couplings.shape[1:]
    )
    (outflow, product), _ = lax.scan(
        sweep_step, (initial, identity), (sources, couplings), reverse=from_right
    )
    inflow = incoming(product, outflow, from_right)
    _, filled = lax.scan(sweep_fill, inflow, (sources, couplings), reverse=from_right)
    return filled


def local(state, advect, viscous, inverse, lower, upper, blades, harmonic):
    fourier_components = harmonic.shape[0]
    derive, frequency, forward_lag_angle, rearward_displacement = spectral_tables(
        blades, harmonic, fourier_components
    )
    exact = lax.Precision.HIGHEST
    axial = with_halo(state, (("seg", 0),), 1, False)
    pitched = with_halo(state, (("pitch", 1),), 1, True)
    slab_index = lax.axis_index("pitch")
    last_slab = lax.axis_size("pitch") - 1
    ghost_low = pitched[:, 0]
    ghost_high = pitched[:, -1]
    ghost_low = jnp.where(
        slab_index == 0,
        jnp.einsum("nm,zvmr->zvnr", rearward_displacement, ghost_low, precision=exact),
        ghost_low,
    )
    ghost_high = jnp.where(
        slab_index == last_slab,
        jnp.einsum("nm,zvmr->zvnr", forward_lag_angle, ghost_high, precision=exact),
        ghost_high,
    )
    lowside = jnp.concatenate([ghost_low[:, None], state[:, :-1]], axis=1)
    highside = jnp.concatenate([state[:, 1:], ghost_high[:, None]], axis=1)
    axial_term = advect[:, :, :, None, :] * (axial[:-2] - axial[2:])
    pitch_term = viscous[:, :, :, None, :] * (lowside + highside - 2.0 * state)
    timing = frequency * jnp.einsum("nm,zpvmr->zpvnr", derive, state, precision=exact)
    residual = axial_term + pitch_term - timing
    scaled = apply_block(inverse.astype(jnp.float32), residual)
    sweep_rows = line_sweep(scaled, lower, False)
    return line_sweep(sweep_rows, upper, True)


def solution(mesh):
    return jax.shard_map(
        local,
        mesh=mesh,
        in_specs=(
            P("seg", "pitch", None, None, None),
            P("seg", "pitch", None, None),
            P("seg", "pitch", None, None),
            P("seg", "pitch", None, None, None),
            P("seg", "pitch", None, None, None),
            P("seg", "pitch", None, None, None),
            P(),
            P(),
        ),
        out_specs=P("seg", "pitch", None, None, None),
        check_vma=False,
    )
```

profile of v0, /device:TPU:1, one launch (start us, length us, event | category | flops | bytes accessed | tf_op | source)
XLA Modules:
  0.0 946.9 jit_solution(1729500404292622695)
XLA Ops:
  6.5 2.7 copy.97
  12.8 2.1 collective-permute-start.2
  19.2 4.6 collective-permute-start
  24.1 2.1 collective-permute-start.1
  30.0 4.8 cosine_reduce_fusion
  34.8 6.3 fusion.2
  41.1 16.9 %collective-permute-done.2 = f32[16,1,5,49,128]{4,0,3,2,1:T(8,128)} collective-permute-done((f32[16,1,5,49,128]{4,0,3,2,1:T(8,128)}, f32[16,1,5,49,128]{4,0,3,2,1:T(8,128)}, u32[]{:S(2)}, u32[]{:S(2)}) %collective-permute-start.2) | collective-permute-done | bytes 2007072 | tf_op jit(solution)/shard_map/ppermute | solution.py:33
  58.1 4.3 fusion.12
  62.4 4.3 fusion.10
  66.8 2.0 fusion.15
  68.7 2.1 fusion.14
  72.1 8.1 multiply_reduce_fusion.8
  80.2 4.0 copy.115
  84.3 42.5 %while.88 = (s32[]{:T(128)}, f32[2,5,49,128]{3,0,2,1:T(2,128)S(1)}, f32[2,5,5,128]{3,0,2,1:T(2,128)S(1)}, f32[16,2,5,49,128]{4,1,3,2,0:T(2,128)}, f32[16,2,5,5,128]{4,1,3,2,0:T(2,128)}, /*index=5*/s32[]{:T(128)}, s32[]{:T(128)}) while((s32[]{:T(128)}, f32[2,5,49,128]{3,0,2,1:T(2,128)S(1)}, f32[2,5,5,128]{3,0,2,1:T(2,128)S(1)}, ...), condition=%wide.region_6.7_spmd.clone, body=%wide.region_3.6_spmd.clone.sunk | while | flops 747523 | bytes 1961055 | solution.py:111
  128.4 81.5 %all-gather.9.cloned.1.call-done = f32[128,5,5,128]{3,2,1,0:T(8,128)} async-done(((f32[2,5,5,128]{3,2,1,0:T(8,128)}), f32[128,5,5,128]{3,2,1,0:T(8,128)}) %all-gather.9.cloned.1.call-update) | async-done | bytes 1638416 | tf_op jit(solution)/shard_map/all_gather | solution.py:13
  209.9 2.6 copy.118
  212.5 101.0 %all-gather.11.cloned.1.call-done = f32[128,5,49,128]{3,2,1,0:T(8,128)} async-done(((f32[2,5,49,128]{3,2,1,0:T(8,128)}), f32[128,5,49,128]{3,2,1,0:T(8,128)}) %all-gather.11.cloned.1.call-update) | async-done | bytes 16056336 | tf_op jit(solution)/shard_map/all_gather | solution.py:13
  313.4 23.3 %copy.119 = f32[64,2,5,49,128]{4,1,3,2,0:T(2,128)} copy(f32[64,2,5,49,128]{4,3,2,1,0:T(8,128)} %bitcast.103) | data formatting | bytes 32112640 | tf_op jit(solution)/shard_map/while | solution.py:22
  338.5 3.0 broadcast.77.clone
  341.6 68.0 %while.85 = (s32[]{:T(128)}, f32[2,5,49,128]{3,0,2,1:T(2,128)S(1)}, f32[16,2,5,49,128]{4,1,3,2,0:T(2,128)}, f32[16,2,5,49,128]{4,1,3,2,0:T(2,128)}, f32[16,2,5,5,128]{4,1,3,2,0:T(2,128)}, /*index=5*/s32[]{:T(128)}) while((s32[]{:T(128)}, f32[2,5,49,128]{3,0,2,1:T(2,128)S(1)}, f32[16,2,5,49,128]{4,1,3,2,0:T(2,128)}, ...), condition=%wide.region_12.13_spmd, body=%wide.region_10.12_spmd.sunk | while | flops 689922 | bytes 2084429 | solution.py:115
  347.2 1.8 fusion.90
  351.4 1.8 fusion.90
  355.7 1.8 fusion.90
  359.9 1.8 fusion.90
  364.2 1.8 fusion.90
  368.4 1.8 fusion.90
  372.7 1.8 fusion.90
  376.9 1.8 fusion.90
  389.7 1.8 fusion.90
  393.9 1.8 fusion.90
  398.2 1.8 fusion.90
  402.4 1.8 fusion.90
  409.6 42.6 %while.89 = (s32[]{:T(128)}, f32[2,5,49,128]{3,0,2,1:T(2,128)S(1)}, f32[2,5,5,128]{3,0,2,1:T(2,128)S(1)}, f32[16,2,5,49,128]{4,1,3,2,0:T(2,128)}, f32[16,2,5,5,1...) while((s32[]{:T(128)}, f32[2,5,49,128]{3,0,2,1:T(2,128)S(1)}, ...), condition=%wide.region_16.17_spmd.clone, body=%wide.region_13.16_spmd.clone.sunk | while | flops 747524 | bytes 1961075 | solution.py:111
  453.7 180.2 %all-gather.13.cloned.1.call-done = f32[128,5,5,128]{3,2,1,0:T(8,128)} async-done(((f32[2,5,5,128]{3,2,1,0:T(8,128)}), f32[128,5,5,128]{3,2,1,0:T(8,128)}) %all-gather.13.cloned.1.call-update) | async-done | bytes 1638416 | tf_op jit(solution)/shard_map/all_gather | solution.py:13
  633.9 2.6 copy.123
  636.5 100.8 %all-gather.15.cloned.1.call-done = f32[128,5,49,128]{3,2,1,0:T(8,128)} async-done(((f32[2,5,49,128]{3,2,1,0:T(8,128)}), f32[128,5,49,128]{3,2,1,0:T(8,128)}) %all-gather.15.cloned.1.call-update) | async-done | bytes 16056336 | tf_op jit(solution)/shard_map/all_gather | solution.py:13
  737.3 23.3 %copy.124 = f32[64,2,5,49,128]{4,1,3,2,0:T(2,128)} copy(f32[64,2,5,49,128]{4,3,2,1,0:T(8,128)} %bitcast.104) | data formatting | bytes 32112640 | tf_op jit(solution)/shard_map/while | solution.py:22
  760.6 108.9 %while.86 = (s32[]{:T(128)}, f32[2,5,49,128]{3,0,2,1:T(2,128)S(1)}, s32[]{:T(128)}, f32[64,2,5,5,128]{4,1,3,2,0:T(2,128)S(1)}, f32[64,2,5,49,128]{4,1,3,2,0:T(2,...) while((s32[]{:T(128)}, f32[2,5,49,128]{3,0,2,1:T(2,128)S(1)}, s32[]{:T(128)}, ...), condition=%wide.region_19.20_spmd, body=%wide.region_17.19_spmd.sunk | while | flops 627206 | bytes 1331347 | solution.py:22
  869.5 3.0 broadcast.77
  872.5 67.9 %while.87 = (s32[]{:T(128)}, f32[2,5,49,128]{3,0,2,1:T(2,128)S(1)}, f32[16,2,5,49,128]{4,1,3,2,0:T(2,128)}, f32[16,2,5,49,128]{4,1,3,2,0:T(2,128)}, f32[16,2,5,5,128]{4,1,3,2,0:T(2,128)}, /*index=5*/s32[]{:T(128)}, s32[]{:T(128)}) while((s32[]{:T(128)}, f32[2,5,49,128]{3,0,2,1:T(2,128)S(1)}, f32[16,2,5,49,128]{4,1,3,2,0:T(2,128)}, ...), condition=%wide.region_22.23_spmd, body=%wide.region_20.22_spmd.sunk | while | flops 689923 | bytes 2083941 | solution.py:115
  873.9 1.8 fusion.91
  882.3 1.8 fusion.91
  886.6 1.8 fusion.91
  899.3 1.8 fusion.91
  903.6 1.8 fusion.91
  916.3 1.8 fusion.91
  920.5 1.8 fusion.91
  933.3 1.8 fusion.91
  (540 shorter events, 307.8 us)
Async XLA Ops:
  6.5 203.3 %all-gather.9.cloned.1.call-start = ((), (), s32[]{:S(2)}) async-start(), calls=%async_computation | async-start | bytes 2662400 | tf_op jit(solution)/shard_map/all_gather | solution.py:13
  9.3 2.0 copy-start
  11.2 5.2 copy-start.2
  12.8 13.4 %copy-start.5 = (s32[2]{0:T(128)S(1)}, s32[2]{0:T(128)}, u32[]{:S(2)}) copy-start(s32[2]{0:T(128)} %param.26) | copy-start | bytes 28
  12.8 15.4 %copy-start.4 = (bf16[16,2,5,5,128]{4,1,3,2,0:T(2,128)(2,1)S(1)}, bf16[16,2,5,5,128]{4,1,3,2,0:T(2,128)(2,1)}, u32[]{:S(2)}) copy-start(bf16[16,2,5,5,128]{4,1,3,2,0:T(2,128)(2,1)} %param.23) | copy-start | bytes 614404
  12.8 17.2 %copy-start.6 = (s32[24]{0:T(128)S(1)}, s32[24]{0:T(128)}, u32[]{:S(2)}) copy-start(s32[24]{0:T(128)} %param.27) | copy-start | bytes 292
  12.8 45.3 %collective-permute-start.2 = (f32[16,1,5,49,128]{4,0,3,2,1:T(8,128)}, f32[16,1,5,49,128]{4,0,3,2,1:T(8,128)}, u32[]{:S(2)}, u32[]{:S(2)}) collective-permute-start(f32[16,1,5,49,128]{4,0,3,2,1:T(8,128)} %copy.102), channel_id=1, source_target_pairs={{0,1},{1,2},{2,3},{3,0},{4,5},{5,6},{6,7},{7,4},{8,9},{9,10},{10,1... | collective-permute-start | bytes 6021128 | tf_op jit(solution)/shard_map/ppermute | solution.py:33
  16.4 46.0 %collective-permute-start.3 = (f32[16,1,5,49,128]{4,0,3,2,1:T(8,128)}, f32[16,1,5,49,128]{4,0,3,2,1:T(8,128)}, u32[]{:S(2)}, u32[]{:S(2)}) collective-permute-start(f32[16,1,5,49,128]{4,0,3,2,1:T(8,128)} %copy.107), channel_id=1, source_target_pairs={{1,0},{2,1},{3,2},{0,3},{5,4},{6,5},{7,6},{4,7},{9,8},{10,9},{11,1... | collective-permute-start | bytes 6021128 | tf_op jit(solution)/shard_map/ppermute | solution.py:35
  19.2 51.7 %collective-permute-start = (f32[1,2,5,49,128]{4,0,2,1,3:T(1,128)S(1)}, f32[1,2,5,49,128]{4,0,2,1,3:T(1,128)S(1)}, u32[]{:S(2)}, u32[]{:S(2)}) collective-permute-start(f32[1,2,5,49,128]{4,0,2,1,3:T(1,128)S(1)} %copy.96), channel_id=1, source_target_pairs={{0,4},{4,8},{8,12},{12,16},{16,20},{20,24},{24,28},{28,32},{32,36}... | collective-permute-start | bytes 752648 | tf_op jit(solution)/shard_map/ppermute | solution.py:33
  24.1 46.8 %collective-permute-start.1 = (f32[1,2,5,49,128]{4,0,2,1,3:T(1,128)S(1)}, f32[1,2,5,49,128]{4,0,2,1,3:T(1,128)S(1)}, u32[]{:S(2)}, u32[]{:S(2)}) collective-permute-start(f32[1,2,5,49,128]{4,0,2,1,3:T(1,128)S(1)} %copy.98), channel_id=1, source_target_pairs={{4,0},{8,4},{12,8},{16,12},{20,16},{24,20},{28,24},{32,28},{36,32}... | collective-permute-start | bytes 752648 | tf_op jit(solution)/shard_map/ppermute | solution.py:35
  68.7 2.7 copy-start.1
  68.7 3.4 copy-start.3
  127.5 185.9 %all-gather.11.cloned.1.call-start = ((), (), s32[]{:S(2)}) async-start(), calls=%async_computation.1 | async-start | bytes 18636800 | tf_op jit(solution)/shard_map/all_gather | solution.py:13
  128.3 505.6 %all-gather.13.cloned.1.call-start = ((), (), s32[]{:S(2)}) async-start(), calls=%async_computation.2 | async-start | bytes 2662400 | tf_op jit(solution)/shard_map/all_gather | solution.py:13
  452.9 284.5 %all-gather.15.cloned.1.call-start = ((), (), s32[]{:S(2)}) async-start(), calls=%async_computation.3 | async-start | bytes 18636800 | tf_op jit(solution)/shard_map/all_gather | solution.py:13
Sparse Core Ops, SparseCore 0:
  127.6 82.2 all-gather.8
  212.6 100.7 all-gather.10
  453.0 180.8 all-gather.12
  636.5 100.7 all-gather.14
where the time goes:
time: 957 us; the launch traced here: 947 us
  waiting for transfers between devices  481 us (50%)
  other arithmetic  295 us (31%)
  local copies, waits for them, and re-layouts  126 us (13%)
  matrix products  15 us (2%)
  between operations  14.8 us (2%)
  starting transfers between devices  10.4 us (1%)
    all_gather x4, waiting for transfers between devices, prefix_2(): gathered = jax.tree.map(lambda a: lax.all_gather(a, axis), part)  464 us
    reduce_sum x160, other arithmetic, apply_block(): jnp.sum(left[..., :, :, None, :] * right[..., None, :, :, :], axis=-3)  88.4 us
    add x63, other arithmetic, combine(): apply_block(later[0], earlier[1]) + later[1]  68.2 us
    dynamic_update_slice x32, other arithmetic, line_sweep(): lax.scan(sweep_fill, inflow, (sources, couplings), reverse=from_right)  57 us
    while x4, local copies, waits for them, and re-layouts, prefix_2(): return lax.fori_loop(0, ahead, one, state)  51.7 us
    mul x127, local copies, waits for them, and re-layouts, apply_block(): left[..., :, :, None, :] * right[..., None, :, :, :]  48.6 us
    add x32, other arithmetic, sweep_step(): current = source_cell + apply_block(coupling_cell, current)  34.7 us
    add x32, other arithmetic, sweep_fill(): current = source_cell + apply_block(coupling_cell, current)  34.4 us
  transfers between devices with their start and end apart: 8, of which 5 were waited for; matrix products, arithmetic and copies ran while one was open for 4% of the time, Pallas kernels for 0%

commit v1 on v0

v1 whole, which is shorter than its diff:
```python
import functools
import math

import jax
import jax.numpy as jnp
import numpy as np
from jax import lax
from jax.experimental import pallas as pl
from jax.experimental.pallas import tpu as pltpu
from jax.sharding import PartitionSpec as P

MESH = pl.DeviceIdType.MESH
ANY = pl.BlockSpec(memory_space=pl.ANY)
V = 5
R = 128
PACK = 64
F32 = jnp.float32


def tables(nt):
    harm = (nt - 1) // 2
    n = np.arange(nt)
    diff = n[:, None] - n[None, :]
    derive = np.where(diff == 0, 0.0, 0.5 * (1 - 2 * (diff % 2)) / np.where(diff == 0, 1.0, np.sin(np.pi * diff / nt)))
    angle = 2 * np.pi * ((n[:, None] * np.arange(1, harm + 1)[None, :]) % nt) / nt
    cosine, sine = np.cos(angle), np.sin(angle)
    rows = 56
    x = np.zeros((rows, R))
    y = np.zeros((rows, R))
    x[:nt, 0] = 1.0 / nt
    x[:nt, 1 : harm + 1], x[:nt, harm + 1 : nt] = 2 * cosine / nt, 2 * sine / nt
    y[:nt, 1 : harm + 1], y[:nt, harm + 1 : nt] = -2 * sine / nt, 2 * cosine / nt
    right = np.zeros((R, 2 * R))
    wide = np.zeros((rows, 2 * R))
    for third in range(3):
        at = slice(third * PACK, third * PACK + nt)
        right[0, at] = 1.0
        right[1 : harm + 1, at], right[harm + 1 : nt, at] = cosine.T, sine.T
        wide[:nt, at] = derive
    return tuple(np.asarray(a, np.float32) for a in (x, y, right, wide))


def bc(tile, k):
    return jnp.broadcast_to(tile[k : k + 1, :], (8, R))


def total(terms):
    terms = list(terms)
    while len(terms) > 1:
        terms = [a + b for a, b in zip(terms[::2], terms[1::2])] + ([terms[-1]] if len(terms) % 2 else [])
    return terms[0]


def matvec(row, vec):
    return [total([row(a, k) * vec[k] for k in range(V)]) for a in range(V)]


def colvec(cols, vec):
    return total([cols[k] * bc(vec, k) for k in range(V)])


def colmat(cols, mat):
    return [colvec(cols, m) for m in mat]


def plus(a, b):
    return [x + y for x, y in zip(a, b)]


def kernel(
    nx, nz, ny, cells, nt,
    state, advect, viscous, inverse, lower, upper, row, ex, ey, eright, ewide,
    out,
    st, pit, ghost, work, adv, vis, inv16, inv, low, upp, rowv, exv, eyv, erv, ewv, wder, wghost,
    pres, qres, mloc, cmat, zmat, resp, xmat,
    csend, cbuf, zsend, zbuf, sol, xbuf, sx, ysend, ybuf, fsend, infl,
    ld, axs, axr, pits, pitr, mcs, mcr, mzs, mzr, mxs, mxr,
    cs, cr, zs, zr, xs, xr, ys, yr, fs, fr, outs,
):
    tiles = (nt + 7) // 8
    last = nt - 8 * (tiles - 1)
    seg = lax.axis_index("seg")
    y = lax.axis_index("pitch")
    core = lax.rem(seg, 2)
    z = lax.rem(seg // 2, nz)
    x = seg // (2 * nz)
    nseg = 2 * nx * nz
    mate = seg + 1 - 2 * core
    yup, ydn = lax.rem(y + 1, ny), lax.rem(y + ny - 1, ny)

    def zpeer(i):
        zz = lax.rem(z + i, nz)
        return zz, (x * nz + zz) * 2 + core

    def xpeer(i):
        xx = lax.rem(x + i, nx)
        return xx, (xx * nz + z) * 2 + core

    def remote(src, dst, send, recv, **to):
        return pltpu.make_async_remote_copy(
            src_ref=src, dst_ref=dst, send_sem=send, recv_sem=recv, device_id=to, device_id_type=MESH
        )

    @pl.loop(0, cells + 2)
    def _(c):
        for p in range(2):
            for v in range(V):
                st[c, p, v, pl.ds(nt, 8 * tiles - nt), :] = jnp.zeros((8 * tiles - nt, R), F32)

    loads = [
        pltpu.make_async_copy(row, rowv, ld.at[0]),
        pltpu.make_async_copy(ex, exv, ld.at[1]),
        pltpu.make_async_copy(ey, eyv, ld.at[2]),
        pltpu.make_async_copy(eright, erv, ld.at[3]),
        pltpu.make_async_copy(ewide, ewv, ld.at[4]),
        pltpu.make_async_copy(state, st.at[pl.ds(1, cells), :, :, pl.ds(0, nt), :], ld.at[5]),
        pltpu.make_async_copy(lower, low, ld.at[6]),
        pltpu.make_async_copy(upper, upp, ld.at[7]),
        pltpu.make_async_copy(advect, adv, ld.at[8]),
        pltpu.make_async_copy(viscous, vis, ld.at[9]),
        pltpu.make_async_copy(inverse, inv16, ld.at[10]),
    ]
    for c in loads:
        c.start()

    barrier = pltpu.get_barrier_semaphore()

    def greet(**to):
        pl.semaphore_signal(barrier, inc=1, device_id=to, device_id_type=MESH)

    greet(pitch=yup)
    greet(pitch=ydn)
    greet(seg=mate)
    greet(seg=lax.rem(seg + 1, nseg))
    greet(seg=lax.rem(seg + nseg - 1, nseg))

    @pl.loop(1, nz)
    def _(i):
        greet(seg=zpeer(i)[1])

    @pl.loop(1, nx)
    def _(i):
        greet(seg=xpeer(i)[1])

    pl.semaphore_wait(barrier, 5 + nz - 1 + nx - 1)

    def rows_of(k):
        return pl.ds(8 * (tiles - 1), last) if k == 0 else pl.ds(8 * (k - 1), 8)

    def pitch_copy(k, d, raw, cellrange=None):
        at = rows_of(k)
        zr_ = pl.ds(0, cells) if cellrange is None else cellrange
        src = state.at[zr_, 1 - d, :, at, :] if raw else ghost.at[zr_, :, at, :]
        return remote(
            src, pit.at[d, zr_, :, at, :], pits.at[d, k], pitr.at[d, k], pitch=yup if d == 0 else ydn
        )

    for d in range(2):
        wraps = (y == ny - 1) if d == 0 else (y == 0)

        @pl.when(jnp.logical_not(wraps))
        def _():
            for k in range(tiles):
                pitch_copy(k, d, True).start()

    ax_up = remote(state.at[cells - 1], st.at[0, :, :, pl.ds(0, nt), :], axs.at[0], axr.at[0], seg=lax.rem(seg + 1, nseg))
    ax_dn = remote(
        state.at[0], st.at[cells + 1, :, :, pl.ds(0, nt), :], axs.at[1], axr.at[1], seg=lax.rem(seg + nseg - 1, nseg)
    )

    @pl.when(seg < nseg - 1)
    def _():
        ax_up.start()

    @pl.when(seg > 0)
    def _():
        ax_dn.start()

    for edge, cell in ((seg == 0, 0), (seg == nseg - 1, cells + 1)):

        @pl.when(edge)
        def _():
            for p in range(2):
                for v in range(V):
                    st[cell, p, v, pl.ds(0, nt), :] = jnp.zeros((nt, R), F32)

    def split3(wide):
        high = wide.astype(jnp.bfloat16)
        low_ = (wide - high.astype(F32)).astype(jnp.bfloat16)
        lane = lax.broadcasted_iota(jnp.int32, wide.shape, 1)
        return jnp.where(lane < 2 * PACK, high.astype(F32), low_.astype(F32)).astype(jnp.bfloat16)[:, : 3 * PACK]

    def stacked(cell):
        s = jnp.concatenate([cell, jnp.zeros((PACK - 8 * tiles, R), F32)], 0)
        high = s.astype(jnp.bfloat16)
        low_ = (s - high.astype(F32)).astype(jnp.bfloat16)
        return jnp.concatenate([high, low_, high], 0)

    def pair(weights, c, p, v):
        rhs = jnp.concatenate([stacked(st[1 + c, p, v]), stacked(st[2 + c, p, v])], 1)
        both = jnp.dot(weights[...], rhs, preferred_element_type=F32)
        return both[:, :R], both[:, R:]

    for c in loads[:6]:
        c.wait()

    @pl.when((y == 0) | (y == ny - 1))
    def _():
        sign = jnp.where(y == 0, 1.0, -1.0).astype(F32)
        e = exv[...] * rowv[pl.ds(0, 1), :] + eyv[...] * (rowv[pl.ds(1, 1), :] * sign)
        wghost[...] = split3(jnp.dot(e, erv[...], precision=lax.Precision.HIGHEST, preferred_element_type=F32))
        p = jnp.where(y == 0, 0, 1)

        @pl.loop(0, cells // 2)
        def _(h):
            for v in range(V):
                a, b = pair(wghost, 2 * h, p, v)
                ghost[2 * h, v] = a
                ghost[2 * h + 1, v] = b
            for d in range(2):

                @pl.when((y == ny - 1) if d == 0 else (y == 0))
                def _():
                    for k in range(2):
                        pitch_copy(k, d, False, pl.ds(2 * h, 2)).start()

        for d in range(2):

            @pl.when((y == ny - 1) if d == 0 else (y == 0))
            def _():
                for k in range(2, tiles):
                    pitch_copy(k, d, False).start()

    for c in loads[6:]:
        c.wait()

    sub = lax.broadcasted_iota(jnp.int32, (8, R), 0)
    unit = [jnp.where(sub == v, 1.0, 0.0).astype(F32) for v in range(V)]
    zero = jnp.zeros((8, R), F32)

    def rowsof(ref, c, p):
        return lambda a, k: ref[c, p, a, pl.ds(k, 1), :]

    def forward_h(c, carry):
        new = []
        for p in range(2):
            h = matvec(rowsof(low, c, p), carry[p])
            for a in range(V):
                pres[c, p, a] = h[a]
            new.append(h)
        return new

    tail = lax.fori_loop(0, cells, forward_h, [list(unit), list(unit)])
    for p in range(2):
        for a in range(V):
            mloc[p, 0, a] = tail[p][a]

    def backward_h(i, carry):
        c = cells - 1 - i
        new = []
        for p in range(2):
            u = rowsof(upp, c, p)
            pu = plus(matvec(u, carry[p][0]), [pres[c, p, a] for a in range(V)])
            qu = matvec(u, carry[p][1])
            for a in range(V):
                pres[c, p, a] = pu[a]
                qres[c, p, a] = qu[a]
            new.append([pu, qu])
        return new

    head = lax.fori_loop(0, cells, backward_h, [[[zero] * V, list(unit)] for _ in range(2)])
    for p in range(2):
        for a in range(V):
            mloc[p, 1, a] = head[p][1][a]
            mloc[p, 2, a] = head[p][0][a]
    mat_core = remote(mloc.at[1 - core], cmat.at[core], mcs, mcr, seg=mate)
    mat_core.start()

    @pl.loop(0, 3)
    def _(m):
        for a in range(V):
            cmat[core, m, a] = mloc[core, m, a]

    @pl.loop(0, cells)
    def _(c):
        for p in range(2):
            for a in range(V):
                inv[c, p, a] = inv16[c, p, a].astype(F32)

    remote(mloc.at[0], cmat.at[1 - core], mcs, mcr, seg=mate).wait_recv()

    def cm(c, m):
        return lambda a, k: cmat[c, m, a, pl.ds(k, 1), :]

    def cvals(c, m):
        return [cmat[c, m, a] for a in range(V)]

    chip_a = matvec(cm(1, 0), cvals(0, 0))
    chip_b = matvec(cm(0, 1), cvals(1, 1))
    chip_c = plus(matvec(cm(0, 1), matvec(cm(1, 2), cvals(0, 0))), cvals(0, 2))
    for m, mat in enumerate((chip_a, chip_b, chip_c)):
        for a in range(V):
            zmat[z, pl.ds(40 * m + a, V, stride=8), :] = mat[a][:V]

    def zm_copy(i, to):
        return remote(zmat.at[z], zmat.at[z], mzs.at[i], mzr.at[z], seg=to)

    @pl.loop(1, nz)
    def _(i):
        zm_copy(i, zpeer(i)[1]).start()

    wder[...] = split3(ewv[...] * rowv[pl.ds(2, 1), pl.ds(0, 1)])

    @pl.when(seg > 0)
    def _():
        ax_up.wait_recv()

    @pl.when(seg < nseg - 1)
    def _():
        ax_dn.wait_recv()

    @pl.loop(0, cells // 2)
    def _(h):
        for p in range(2):
            for v in range(V):
                timing = pair(wder, 2 * h, p, v)
                for j in range(2):
                    c = 2 * h + j
                    a1 = adv[c, p, pl.ds(v, 1), :]
                    v1 = vis[c, p, pl.ds(v, 1), :]
                    work[c, p, v] = (
                        a1 * (st[c, p, v] - st[c + 2, p, v])
                        + v1 * (st[c + 1, 1 - p, v] - 2.0 * st[c + 1, p, v])
                        - timing[j]
                    )

    def cols(ref, i, m):
        return [ref[i, pl.ds(40 * m + 8 * j, 8), :] for j in range(V)]

    def put(ref, i, m, mat):
        for j in range(V):
            ref[i, pl.ds(40 * m + 8 * j, 8), :] = mat[j]

    def z_responses():
        @pl.loop(1, nz)
        def _(i):
            zz, _s = zpeer(i)
            remote(zmat.at[zz], zmat.at[zz], mzs.at[i], mzr.at[zz], seg=mate).wait_recv()

        def ahead(d, s):
            put(resp, d, 0, s)
            return colmat(cols(zmat, d, 0), s)

        s_end = lax.fori_loop(0, nz, ahead, list(unit))

        def back(i, carry):
            d = nz - 1 - i
            pu, qu = carry
            put(resp, d, 1, pu)
            put(resp, d, 2, qu)
            b = cols(zmat, d, 1)
            return [plus(colmat(b, pu), colmat(cols(zmat, d, 2), cols(resp, d, 0))), colmat(b, qu)]

        pu, qu = lax.fori_loop(0, nz, back, [[zero] * V, list(unit)])
        put(xmat, x, 0, s_end)
        put(xmat, x, 1, qu)
        put(xmat, x, 2, pu)

        @pl.loop(1, nx)
        def _(i):
            remote(xmat.at[x], xmat.at[x], mxs.at[i], mxr.at[x], seg=xpeer(i)[1]).start()

    def x_responses():
        @pl.loop(1, nx)
        def _(i):
            xx, _s = xpeer(i)
            remote(xmat.at[xx], xmat.at[xx], mxs.at[i], mxr.at[xx], seg=mate).wait_recv()

    def tile_rows(k):
        t = lax.rem(k + tiles - 1, tiles)
        return pl.ds(pl.multiple_of(8 * t, 8), 8)

    def stage_local(k):
        at = tile_rows(k)
        for d in range(2):

            @pl.when(k == 0)
            def _():
                pitch_copy(0, d, True).wait_recv()

            @pl.when(k > 0)
            def _():
                src = state.at[:, 0, :, pl.ds(0, 8), :]
                remote(src, pit.at[d, :, :, pl.ds(0, 8), :], pits.at[d, k], pitr.at[d, k], pitch=yup).wait_recv()

        def ahead(c, carry):
            new = []
            for p in range(2):
                r = [work[c, p, v, at, :] + vis[c, p, pl.ds(v, 1), :] * pit[p, c, v, at, :] for v in range(V)]
                s = plus(matvec(rowsof(inv, c, p), r), matvec(rowsof(low, c, p), carry[p]))
                for a in range(V):
                    work[c, p, a, at, :] = s[a]
                new.append(s)
            return new

        ends = lax.fori_loop(0, cells, ahead, [[zero] * V for _ in range(2)])

        def back(i, carry):
            c = cells - 1 - i
            new = []
            for p in range(2):
                u = plus(matvec(rowsof(upp, c, p), carry[p]), [work[c, p, a, at, :] for a in range(V)])
                for a in range(V):
                    work[c, p, a, at, :] = u[a]
                new.append(u)
            return new

        heads = lax.fori_loop(0, cells, back, [[zero] * V for _ in range(2)])
        for p in range(2):
            for a in range(V):
                csend[k, p, a] = ends[p][a]
                csend[k, p, V + a] = heads[p][a]
        remote(csend.at[k, 1 - core], cbuf.at[k, core], cs.at[k], cr.at[k], seg=mate).start()
        for a in range(2 * V):
            cbuf[k, core, a] = csend[k, core, a]

    def stage_chip(k):
        remote(csend.at[k, 0], cbuf.at[k, 1 - core], cs.at[k], cr.at[k], seg=mate).wait_recv()
        b0, c0, b1, c1 = ([cbuf[k, c, o + a] for a in range(V)] for c in range(2) for o in (0, V))
        b = plus(matvec(cm(1, 0), b0), b1)
        c = plus(matvec(cm(0, 1), plus(matvec(cm(1, 2), b0), c1)), c0)
        for a in range(V):
            zsend[k, pl.ds(a, 8, stride=16), :] = b[a]
            zsend[k, pl.ds(8 + a, 8, stride=16), :] = c[a]

        @pl.loop(1, nz)
        def _(i):
            zz, to = zpeer(i)
            src = zsend.at[k, pl.ds(pl.multiple_of(16 * zz, 16), 16), :]
            remote(src, zbuf.at[k, z], zs.at[k, i], zr.at[k, z], seg=to).start()

        zbuf[k, z] = zsend[k, pl.ds(pl.multiple_of(16 * z, 16), 16), :]

    def half(ref, k, d, o):
        return ref[k, d, pl.ds(8 * o, 8), :]

    def stage_z(k):
        @pl.loop(1, nz)
        def _(i):
            zz, _s = zpeer(i)
            remote(zsend.at[k, pl.ds(0, 16), :], zbuf.at[k, zz], zs.at[k, i], zr.at[k, zz], seg=mate).wait_recv()

        def ahead(d, s):
            sol[k, d, pl.ds(0, 8), :] = s
            return colvec(cols(zmat, d, 0), s) + half(zbuf, k, d, 0)

        b = lax.fori_loop(0, nz, ahead, zero)

        def back(i, u):
            d = nz - 1 - i
            sol[k, d, pl.ds(8, 8), :] = u
            return (
                colvec(cols(zmat, d, 1), u) + colvec(cols(zmat, d, 2), half(sol, k, d, 0)) + half(zbuf, k, d, 1)
            )

        c = lax.fori_loop(0, nz, back, zero)
        xbuf[k, x, pl.ds(0, 8), :] = b
        xbuf[k, x, pl.ds(8, 8), :] = c

        @pl.loop(1, nx)
        def _(i):
            remote(xbuf.at[k, x], xbuf.at[k, x], xs.at[k, i], xr.at[k, x], seg=xpeer(i)[1]).start()

    def stage_x(k):
        @pl.loop(1, nx)
        def _(i):
            xx, _s = xpeer(i)
            remote(xbuf.at[k, xx], xbuf.at[k, xx], xs.at[k, i], xr.at[k, xx], seg=mate).wait_recv()

        def ahead(d, s):
            sx[d, pl.ds(0, 8), :] = s
            return colvec(cols(xmat, d, 0), s) + half(xbuf, k, d, 0)

        lax.fori_loop(0, nx, ahead, zero)

        def back(i, u):
            d = nx - 1 - i
            sx[d, pl.ds(8, 8), :] = u
            return (
                colvec(cols(xmat, d, 1), u)
                + colvec(cols(xmat, d, 2), sx[d, pl.ds(0, 8), :])
                + half(xbuf, k, d, 1)
            )

        lax.fori_loop(0, nx, back, zero)
        s_in, u_in = sx[x, pl.ds(0, 8), :], sx[x, pl.ds(8, 8), :]
        sb, ub = [bc(s_in, j) for j in range(V)], [bc(u_in, j) for j in range(V)]

        @pl.loop(0, nz)
        def _(d):
            ss, ps, qs = cols(resp, d, 0), cols(resp, d, 1), cols(resp, d, 2)
            ysend[k, d, pl.ds(0, 8), :] = half(sol, k, d, 0) + total([ss[j] * sb[j] for j in range(V)])
            ysend[k, d, pl.ds(8, 8), :] = half(sol, k, d, 1) + total(
                [ps[j] * sb[j] for j in range(V)] + [qs[j] * ub[j] for j in range(V)]
            )

        @pl.loop(1, nz)
        def _(i):
            zz, to = zpeer(i)
            dst = ybuf.at[k, pl.ds(pl.multiple_of(16 * z, 16), 16), :]
            remote(ysend.at[k, zz], dst, ys.at[k, i], yr.at[k, z], seg=to).start()

        ybuf[k, pl.ds(pl.multiple_of(16 * z, 16), 16), :] = ysend[k, z]

    def stage_back(k):
        @pl.loop(1, nz)
        def _(i):
            zz, _s = zpeer(i)
            dst = ybuf.at[k, pl.ds(pl.multiple_of(16 * zz, 16), 16), :]
            remote(ysend.at[k, 0], dst, ys.at[k, i], yr.at[k, zz], seg=mate).wait_recv()

        s0 = [ybuf[k, pl.ds(a, 8, stride=16), :] for a in range(V)]
        u1 = [ybuf[k, pl.ds(8 + a, 8, stride=16), :] for a in range(V)]
        s1 = plus(matvec(cm(0, 0), s0), [cbuf[k, 0, a] for a in range(V)])
        u0 = plus(plus(matvec(cm(1, 1), u1), matvec(cm(1, 2), s1)), [cbuf[k, 1, V + a] for a in range(V)])
        for c, (s, u) in enumerate(((s0, u0), (s1, u1))):
            for a in range(V):
                fsend[k, c, a] = s[a]
                fsend[k, c, V + a] = u[a]
        remote(fsend.at[k, 1 - core], infl.at[k, core], fs.at[k], fr.at[k], seg=mate).start()
        for a in range(2 * V):
            infl[k, core, a] = fsend[k, core, a]

    def out_copy(k, wait):
        at0 = pl.ds(8 * (tiles - 1), last)

        @pl.when(k == 0)
        def _():
            c = pltpu.make_async_copy(work.at[:, :, :, at0, :], out.at[:, :, :, at0, :], outs.at[k])
            c.wait() if wait else c.start()

        @pl.when(k > 0)
        def _():
            at = pl.ds(pl.multiple_of(8 * (jnp.maximum(k, 1) - 1), 8), 8)
            c = pltpu.make_async_copy(work.at[:, :, :, at, :], out.at[:, :, :, at, :], outs.at[k])
            c.wait() if wait else c.start()

    def stage_final(k):
        remote(fsend.at[k, 0], infl.at[k, 1 - core], fs.at[k], fr.at[k], seg=mate).wait_recv()
        at = tile_rows(k)
        s = [[infl[k, p, a] for a in range(V)] for p in range(2)]
        u = [[infl[k, p, V + a] for a in range(V)] for p in range(2)]

        @pl.loop(0, cells)
        def _(c):
            for p in range(2):
                fix = plus(matvec(rowsof(pres, c, p), s[p]), matvec(rowsof(qres, c, p), u[p]))
                for a in range(V):
                    work[c, p, a, at, :] = work[c, p, a, at, :] + fix[a]

        out_copy(k, False)

    @pl.loop(0, tiles + 4)
    def _(step):
        @pl.when(step < tiles)
        def _():
            stage_local(step)
            stage_chip(step)

        @pl.when(step == 1)
        def _():
            z_responses()

        @pl.when((step >= 1) & (step < tiles + 1))
        def _():
            stage_z(step - 1)

        @pl.when(step == 2)
        def _():
            x_responses()

        @pl.when((step >= 2) & (step < tiles + 2))
        def _():
            stage_x(step - 2)

        @pl.when((step >= 3) & (step < tiles + 3))
        def _():
            stage_back(step - 3)

        @pl.when(step >= 4)
        def _():
            stage_final(step - 4)

    @pl.when(seg < nseg - 1)
    def _():
        ax_up.wait_send()

    @pl.when(seg > 0)
    def _():
        ax_dn.wait_send()

    mat_core.wait_send()
    for d in range(2):
        for k in range(tiles):
            pitch_copy(k, d, True).wait_send()

    @pl.loop(1, nz)
    def _(i):
        zm_copy(i, mate).wait_send()

    @pl.loop(1, nx)
    def _(i):
        remote(xmat.at[x], xmat.at[x], mxs.at[i], mxr.at[x], seg=mate).wait_send()

    @pl.loop(0, tiles)
    def _(k):
        remote(csend.at[k, 0], cbuf.at[k, 0], cs.at[k], cr.at[k], seg=mate).wait_send()
        remote(fsend.at[k, 0], infl.at[k, 0], fs.at[k], fr.at[k], seg=mate).wait_send()

        @pl.loop(1, nz)
        def _(i):
            remote(zsend.at[k, pl.ds(0, 16), :], zbuf.at[k, 0], zs.at[k, i], zr.at[k, 0], seg=mate).wait_send()
            remote(ysend.at[k, 0], zbuf.at[k, 0], ys.at[k, i], yr.at[k, 0], seg=mate).wait_send()

        @pl.loop(1, nx)
        def _(i):
            remote(xbuf.at[k, 0], xbuf.at[k, 0], xs.at[k, i], xr.at[k, 0], seg=mate).wait_send()

        out_copy(k, True)


def local(nx, nz, ny, state, advect, viscous, inverse, lower, upper, blades, harmonic):
    cells, _, _, nt, _ = state.shape
    harm = harmonic.shape[0]
    ratio = blades[1].astype(F32) / blades[0].astype(F32)
    lag = 2.0 * math.pi * harmonic.astype(F32) * ratio
    angle = jnp.concatenate([jnp.zeros((1,), F32), lag, lag, jnp.zeros((R - 1 - 2 * harm,), F32)])
    row = jnp.stack([jnp.cos(angle), jnp.sin(angle), jnp.full((R,), ratio / harm)] + [jnp.zeros((R,), F32)] * 5)
    tiles = (nt + 7) // 8
    rows = 8 * tiles
    vm, dma = lambda *s: pltpu.VMEM(s, F32), lambda *s: pltpu.SemaphoreType.DMA(s)
    bf = lambda *s: pltpu.VMEM(s, jnp.bfloat16)
    scratch = [
        vm(cells + 2, 2, V, rows, R), vm(2, cells, V, rows, R), vm(cells, V, rows, R), vm(cells, 2, V, rows, R),
        vm(cells, 2, V, R), vm(cells, 2, V, R), bf(cells, 2, V, V, R), vm(cells, 2, V, V, R),
        vm(cells, 2, V, V, R), vm(cells, 2, V, V, R), vm(8, R), vm(rows, R), vm(rows, R), vm(R, 2 * R), vm(rows, 2 * R),
        bf(rows, 3 * PACK), bf(rows, 3 * PACK),
        vm(cells, 2, V, 8, R), vm(cells, 2, V, 8, R), vm(2, 3, V, 8, R), vm(2, 3, V, 8, R),
        vm(nz, 120, R), vm(nz, 120, R), vm(nx, 120, R),
        vm(tiles, 2, 2 * V, 8, R), vm(tiles, 2, 2 * V, 8, R), vm(tiles, 16 * nz, R), vm(tiles, nz, 16, R),
        vm(tiles, nz, 16, R), vm(tiles, nx, 16, R), vm(nx, 16, R), vm(tiles, nz, 16, R), vm(tiles, 16 * nz, R),
        vm(tiles, 2, 2 * V, 8, R), vm(tiles, 2, 2 * V, 8, R),
        dma(11), dma(2), dma(2), dma(2, tiles), dma(2, tiles), pltpu.SemaphoreType.DMA, pltpu.SemaphoreType.DMA,
        dma(nz), dma(nz), dma(nx), dma(nx),
        dma(tiles), dma(tiles), dma(tiles, nz), dma(tiles, nz), dma(tiles, nx), dma(tiles, nx),
        dma(tiles, nz), dma(tiles, nz), dma(tiles), dma(tiles), dma(tiles),
    ]
    return pl.pallas_call(
        functools.partial(kernel, nx, nz, ny, cells, nt),
        out_shape=jax.ShapeDtypeStruct(state.shape, F32),
        in_specs=[ANY] * 11,
        out_specs=ANY,
        scratch_shapes=scratch,
        compiler_params=pltpu.CompilerParams(collective_id=0, has_side_effects=True),
        name="line_update",
    )(state, advect, viscous, inverse, lower, upper, row, *tables(nt))


def solution(mesh):
    nz = 8
    nx, ny = mesh.shape["seg"] // (2 * nz), mesh.shape["pitch"]
    five, four = P("seg", "pitch", None, None, None), P("seg", "pitch", None, None)
    return jax.shard_map(
        functools.partial(local, nx, nz, ny),
        mesh=mesh,
        in_specs=(five, four, four, five, five, five, P(), P()),
        out_specs=five,
        check_vma=False,
    )
```

time: 957 us -> 102 us (0.11)
  waiting for transfers between devices: 481 us -> 0 us
  other arithmetic: 295 us -> 0.78 us
  local copies, waits for them, and re-layouts: 126 us -> 21.5 us
  Pallas kernels: 0 us -> 77.6 us
  matrix products: 15 us -> 0 us
  between operations: 14.8 us -> 1.36 us
  starting transfers between devices: 10.4 us -> 0 us
    all_gather x4 -> x0, waiting for transfers between devices: 464 us -> none  [prefix_2(): gathered = jax.tree.map(lambda a: lax.all_gather(a, axis), part)]
    add x128 -> x0, other arithmetic: 137 us -> none  [the longest x63 68.2 us: combine(): apply_block(later[0], earlier[1]) + later[1]]
    reduce_sum x161 -> x0, other arithmetic: 93.2 us -> none  [the longest x160 88.4 us: apply_block(): jnp.sum(left[..., :, :, None, :] * right[..., None, :, :, :], axis=-3)]
    pallas_call x0 -> x1, Pallas kernels: none -> 77.6 us  [local(): pl.pallas_call(functools.partial(kernel, nx, nz, ny, cells, nt), out_shap...]
    dynamic_update_slice x32 -> x0, other arithmetic: 57 us -> none  [line_sweep(): lax.scan(sweep_fill, inflow, (sources, couplings), reverse=from_right)]
    while x40 -> x0, local copies, waits for them, and re-layouts: 54.6 us -> none  [the longest x4 51.7 us: prefix_2(): return lax.fori_loop(0, ahead, one, state)]
    mul x127 -> x0, local copies, waits for them, and re-layouts: 48.6 us -> none  [apply_block(): left[..., :, :, None, :] * right[..., None, :, :, :]]
    ppermute x4 -> x0, waiting for transfers between devices: 17 us -> none  [the longest x2 17 us: with_halo(): lax.ppermute(tail, axis, [(i, (i + 1) % count) for i in range(ends)])]
  transfers between devices with their start and end apart: 8 -> 0, of which waited for: 5 -> 0; matrix products, arithmetic and copies ran while one was open for 4% -> 0% of each run, Pallas kernels for 0% -> 0%
where the time goes in v1:
time: 102 us; the launch traced here: 101 us
  Pallas kernels  77.6 us (76%)
  local copies, waits for them, and re-layouts  21.5 us (21%)
  between operations  1.36 us (1%)
    pallas_call x1, Pallas kernels, local(): pl.pallas_call(functools.partial(kernel, nx, nz, ny, cells, nt), out_shap...  77.6 us
    unnamed x6, local copies, waits for them, and re-layouts  13.2 us
    pallas_call x1, local copies, waits for them, and re-layouts, local(): pl.pallas_call(functools.partial(kernel, nx, nz, ny, cells, nt), out_shap...  6.31 us

profile of v1, /device:TPU:1, one launch (start us, length us, event | category | flops | bytes accessed | tf_op | source)
XLA Modules:
  0.0 101.3 jit_solution(17035421201079345866)
XLA Ops:
  0.0 1.3 %fusion.1 = (s32[1]{0:T(128)}, s32[1]{0:T(128)}) fusion(s32[2]{0:T(128)} %param.18), kind=kLoop, calls=%fused_computation.3 | loop fusion | bytes 16 | tf_op jit(solution)/shard_map/slice | solution.py:635
  2.7 0.7 multiply_bitcast_fusion
  3.3 0.1 fusion
  3.5 0.6 stack.9.row
  4.1 1.6 %copy.14.advect = f32[16,2,5,128]{3,2,1,0:T(8,128)} copy(f32[16,2,5,128]{3,1,2,0:T(2,128)} %param.13) | data formatting | bytes 163840 | tf_op args[1]
  5.7 1.6 %copy.15.viscous = f32[16,2,5,128]{3,2,1,0:T(8,128)} copy(f32[16,2,5,128]{3,1,2,0:T(2,128)} %param.14) | data formatting | bytes 163840 | tf_op args[2]
  7.2 1.7 %copy.16.inverse = bf16[16,2,5,5,128]{4,3,2,1,0:T(8,128)(2,1)} copy(bf16[16,2,5,5,128]{4,1,3,2,0:T(2,128)(2,1)} %param.15) | data formatting | bytes 409600 | tf_op args[3]
  8.9 1.9 %copy.17.lower = f32[16,2,5,5,128]{4,3,2,1,0:T(8,128)} copy(f32[16,2,5,5,128]{4,1,3,2,0:T(2,128)} %param.16) | data formatting | bytes 819200 | tf_op args[4]
  10.9 2.0 %copy.18.upper = f32[16,2,5,5,128]{4,3,2,1,0:T(8,128)} copy(f32[16,2,5,5,128]{4,1,3,2,0:T(2,128)} %param.17) | data formatting | bytes 819200 | tf_op args[5]
  12.8 4.5 %copy.13.state = f32[16,2,5,49,128]{4,3,2,1,0:T(8,128)} copy(f32[16,2,5,49,128]{4,1,3,2,0:T(2,128)} %param.12) | data formatting | bytes 8028160 | tf_op args[0]
  17.4 77.6 %line_update.1 = f32[16,2,5,49,128]{4,3,2,1,0:T(8,128)} custom-call(f32[16,2,5,49,128]{4,3,2,1,0:T(8,128)} %copy.13.state, f32[16,2,5,128]{3,2,1,0:T(8,128)} %copy.14.advect, f32[16,2,5,128]{3,2,1,0:T(8,128)} %copy.15.viscous, bf16[16,2,5,5,128]{4,3,2,1,0:T(8,128)(2,1)} %copy.16.inverse, f32[16,2,5,5,128]{4,3,2,1,0:T(8,128)} %copy.17.lower, ...), custom_call_target="tpu_custom_call" | custom-call | tf_op jit(solution)/shard_map/line_update/pallas_call | solution.py:658
  95.0 6.3 %copy.19 = f32[16,2,5,49,128]{4,1,3,2,0:T(2,128)} copy(f32[16,2,5,49,128]{4,3,2,1,0:T(8,128)} %line_update.1) | data formatting | bytes 8028160 | tf_op jit(solution)/shard_map/line_update/pallas_call | solution.py:658
  (5 shorter events, 0.0 us)

commit v2 on v1

--- a/solution.py
+++ b/solution.py
@@ -69,9 +69,9 @@
 
 def kernel(
     nx, nz, ny, cells, nt,
-    state, advect, viscous, inverse, lower, upper, row, ex, ey, eright, ewide,
+    state, advect, viscous, inverse, lower, upper, blades, harmonic, ex, ey, eright, ewide,
     out,
-    st, pit, ghost, work, adv, vis, inv16, inv, low, upp, rowv, exv, eyv, erv, ewv, wder, wghost,
+    st, pit, ghost, work, adv, vis, inv16, inv, low, upp, exv, eyv, erv, ewv, wder, wghost,
     pres, qres, mloc, cmat, zmat, resp, xmat,
     csend, cbuf, zsend, zbuf, sol, xbuf, sx, ysend, ybuf, fsend, infl,
     ld, axs, axr, pits, pitr, mcs, mcr, mzs, mzr, mxs, mxr,
@@ -108,18 +108,21 @@
                 st[c, p, v, pl.ds(nt, 8 * tiles - nt), :] = jnp.zeros((8 * tiles - nt, R), F32)
 
     loads = [
-        pltpu.make_async_copy(row, rowv, ld.at[0]),
-        pltpu.make_async_copy(ex, exv, ld.at[1]),
-        pltpu.make_async_copy(ey, eyv, ld.at[2]),
-        pltpu.make_async_copy(eright, erv, ld.at[3]),
-        pltpu.make_async_copy(ewide, ewv, ld.at[4]),
-        pltpu.make_async_copy(state, st.at[pl.ds(1, cells), :, :, pl.ds(0, nt), :], ld.at[5]),
-        pltpu.make_async_copy(lower, low, ld.at[6]),
-        pltpu.make_async_copy(upper, upp, ld.at[7]),
-        pltpu.make_async_copy(advect, adv, ld.at[8]),
-        pltpu.make_async_copy(viscous, vis, ld.at[9]),
-        pltpu.make_async_copy(inverse, inv16, ld.at[10]),
+        pltpu.make_async_copy(ex, exv, ld.at[0]),
+        pltpu.make_async_copy(ey, eyv, ld.at[1]),
+        pltpu.make_async_copy(eright, erv, ld.at[2]),
+        pltpu.make_async_copy(ewide, ewv, ld.at[3]),
     ]
+    for p in range(2):
+        dst = st.at[pl.ds(1, cells), p, :, pl.ds(0, nt), :]
+        loads.append(pltpu.make_async_copy(state.at[:, :, :, p, :], dst, ld.at[4 + p]))
+    for j, (src, dst) in enumerate(((lower, low), (upper, upp))):
+        for p in range(2):
+            loads.append(pltpu.make_async_copy(src.at[:, :, :, p, :], dst.at[:, p], ld.at[6 + 2 * j + p]))
+    for j, (src, dst) in enumerate(((advect, adv), (viscous, vis))):
+        for p in range(2):
+            loads.append(pltpu.make_async_copy(src.at[:, :, p, :], dst.at[:, p], ld.at[10 + 2 * j + p]))
+    loads.append(pltpu.make_async_copy(inverse, inv16, ld.at[14]))
     for c in loads:
         c.start()
 
@@ -150,7 +153,7 @@
     def pitch_copy(k, d, raw, cellrange=None):
         at = rows_of(k)
         zr_ = pl.ds(0, cells) if cellrange is None else cellrange
-        src = state.at[zr_, 1 - d, :, at, :] if raw else ghost.at[zr_, :, at, :]
+        src = state.at[zr_, :, at, 1 - d, :] if raw else ghost.at[zr_, :, at, :]
         return remote(
             src, pit.at[d, zr_, :, at, :], pits.at[d, k], pitr.at[d, k], pitch=yup if d == 0 else ydn
         )
@@ -163,18 +166,20 @@
             for k in range(tiles):
                 pitch_copy(k, d, True).start()
 
-    ax_up = remote(state.at[cells - 1], st.at[0, :, :, pl.ds(0, nt), :], axs.at[0], axr.at[0], seg=lax.rem(seg + 1, nseg))
-    ax_dn = remote(
-        state.at[0], st.at[cells + 1, :, :, pl.ds(0, nt), :], axs.at[1], axr.at[1], seg=lax.rem(seg + nseg - 1, nseg)
-    )
-
-    @pl.when(seg < nseg - 1)
-    def _():
-        ax_up.start()
-
-    @pl.when(seg > 0)
-    def _():
-        ax_dn.start()
+    def axial(j, p):
+        cell, slot, to = ((cells - 1, 0, seg + 1), (0, cells + 1, seg + nseg - 1))[j]
+        dst = st.at[slot, p, :, pl.ds(0, nt), :]
+        return remote(state.at[cell, :, :, p, :], dst, axs.at[j, p], axr.at[j, p], seg=lax.rem(to, nseg))
+
+    def has_axial(j, receive):
+        return seg > 0 if (j == 0) == receive else seg < nseg - 1
+
+    for j in range(2):
+
+        @pl.when(has_axial(j, False))
+        def _():
+            for p in range(2):
+                axial(j, p).start()
 
     for edge, cell in ((seg == 0, 0), (seg == nseg - 1, cells + 1)):
 
@@ -183,6 +188,8 @@
             for p in range(2):
                 for v in range(V):
                     st[cell, p, v, pl.ds(0, nt), :] = jnp.zeros((nt, R), F32)
+
+    rotor, stator = blades[0].astype(F32), blades[1].astype(F32)
 
     def split3(wide):
         high = wide.astype(jnp.bfloat16)
@@ -207,7 +214,14 @@
     @pl.when((y == 0) | (y == ny - 1))
     def _():
         sign = jnp.where(y == 0, 1.0, -1.0).astype(F32)
-        e = exv[...] * rowv[pl.ds(0, 1), :] + eyv[...] * (rowv[pl.ds(1, 1), :] * sign)
+        lane = lax.broadcasted_iota(jnp.int32, (8, R), 1)
+        mode = jnp.zeros((8, R), F32)
+        for k in range((nt - 1) // 2):
+            hit = (lane == 1 + k) | (lane == 1 + k + (nt - 1) // 2)
+            mode = jnp.where(hit, harmonic[k].astype(F32), mode)
+        turns = mode * stator / rotor
+        angle = (2.0 * math.pi) * (turns - jnp.floor(turns + 0.5))
+        e = exv[...] * jnp.cos(angle)[:1] + eyv[...] * (jnp.sin(angle)[:1] * sign)
         wghost[...] = split3(jnp.dot(e, erv[...], precision=lax.Precision.HIGHEST, preferred_element_type=F32))
         p = jnp.where(y == 0, 0, 1)
 
@@ -283,9 +297,11 @@
 
     @pl.loop(0, cells)
     def _(c):
-        for p in range(2):
-            for a in range(V):
-                inv[c, p, a] = inv16[c, p, a].astype(F32)
+        for a in range(V):
+            for k in range(V):
+                both = inv16[c, a, k].astype(F32)
+                for p in range(2):
+                    inv[c, p, a, pl.ds(k, 1), :] = both[p : p + 1]
 
     remote(mloc.at[0], cmat.at[1 - core], mcs, mcr, seg=mate).wait_recv()
 
@@ -309,15 +325,14 @@
     def _(i):
         zm_copy(i, zpeer(i)[1]).start()
 
-    wder[...] = split3(ewv[...] * rowv[pl.ds(2, 1), pl.ds(0, 1)])
-
-    @pl.when(seg > 0)
-    def _():
-        ax_up.wait_recv()
-
-    @pl.when(seg < nseg - 1)
-    def _():
-        ax_dn.wait_recv()
+    wder[...] = split3(ewv[...] * (jnp.full((1, 2 * R), stator, F32) / jnp.full((1, 2 * R), rotor * ((nt - 1) // 2), F32)))
+
+    for j in range(2):
+
+        @pl.when(has_axial(j, True))
+        def _():
+            for p in range(2):
+                axial(j, p).wait_recv()
 
     @pl.loop(0, cells // 2)
     def _(h):
@@ -390,7 +405,7 @@
 
             @pl.when(k > 0)
             def _():
-                src = state.at[:, 0, :, pl.ds(0, 8), :]
+                src = state.at[:, :, pl.ds(0, 8), 0, :]
                 remote(src, pit.at[d, :, :, pl.ds(0, 8), :], pits.at[d, k], pitr.at[d, k], pitch=yup).wait_recv()
 
         def ahead(c, carry):
@@ -534,16 +549,18 @@
     def out_copy(k, wait):
         at0 = pl.ds(8 * (tiles - 1), last)
 
+        def both(at):
+            for p in range(2):
+                c = pltpu.make_async_copy(work.at[:, p, :, at, :], out.at[:, :, at, p, :], outs.at[k, p])
+                c.wait() if wait else c.start()
+
         @pl.when(k == 0)
         def _():
-            c = pltpu.make_async_copy(work.at[:, :, :, at0, :], out.at[:, :, :, at0, :], outs.at[k])
-            c.wait() if wait else c.start()
+            both(at0)
 
         @pl.when(k > 0)
         def _():
-            at = pl.ds(pl.multiple_of(8 * (jnp.maximum(k, 1) - 1), 8), 8)
-            c = pltpu.make_async_copy(work.at[:, :, :, at, :], out.at[:, :, :, at, :], outs.at[k])
-            c.wait() if wait else c.start()
+            both(pl.ds(pl.multiple_of(8 * (jnp.maximum(k, 1) - 1), 8), 8))
 
     def stage_final(k):
         remote(fsend.at[k, 0], infl.at[k, 1 - core], fs.at[k], fr.at[k], seg=mate).wait_recv()
@@ -591,13 +608,12 @@
         def _():
             stage_final(step - 4)
 
-    @pl.when(seg < nseg - 1)
-    def _():
-        ax_up.wait_send()
-
-    @pl.when(seg > 0)
-    def _():
-        ax_dn.wait_send()
+    for j in range(2):
+
+        @pl.when(has_axial(j, False))
+        def _():
+            for p in range(2):
+                axial(j, p).wait_send()
 
     mat_core.wait_send()
     for d in range(2):
@@ -631,39 +647,39 @@
 
 def local(nx, nz, ny, state, advect, viscous, inverse, lower, upper, blades, harmonic):
     cells, _, _, nt, _ = state.shape
-    harm = harmonic.shape[0]
-    ratio = blades[1].astype(F32) / blades[0].astype(F32)
-    lag = 2.0 * math.pi * harmonic.astype(F32) * ratio
-    angle = jnp.concatenate([jnp.zeros((1,), F32), lag, lag, jnp.zeros((R - 1 - 2 * harm,), F32)])
-    row = jnp.stack([jnp.cos(angle), jnp.sin(angle), jnp.full((R,), ratio / harm)] + [jnp.zeros((R,), F32)] * 5)
     tiles = (nt + 7) // 8
     rows = 8 * tiles
     vm, dma = lambda *s: pltpu.VMEM(s, F32), lambda *s: pltpu.SemaphoreType.DMA(s)
     bf = lambda *s: pltpu.VMEM(s, jnp.bfloat16)
     scratch = [
         vm(cells + 2, 2, V, rows, R), vm(2, cells, V, rows, R), vm(cells, V, rows, R), vm(cells, 2, V, rows, R),
-        vm(cells, 2, V, R), vm(cells, 2, V, R), bf(cells, 2, V, V, R), vm(cells, 2, V, V, R),
-        vm(cells, 2, V, V, R), vm(cells, 2, V, V, R), vm(8, R), vm(rows, R), vm(rows, R), vm(R, 2 * R), vm(rows, 2 * R),
+        vm(cells, 2, V, R), vm(cells, 2, V, R), bf(cells, V, V, 2, R), vm(cells, 2, V, V, R),
+        vm(cells, 2, V, V, R), vm(cells, 2, V, V, R), vm(rows, R), vm(rows, R), vm(R, 2 * R), vm(rows, 2 * R),
         bf(rows, 3 * PACK), bf(rows, 3 * PACK),
         vm(cells, 2, V, 8, R), vm(cells, 2, V, 8, R), vm(2, 3, V, 8, R), vm(2, 3, V, 8, R),
         vm(nz, 120, R), vm(nz, 120, R), vm(nx, 120, R),
         vm(tiles, 2, 2 * V, 8, R), vm(tiles, 2, 2 * V, 8, R), vm(tiles, 16 * nz, R), vm(tiles, nz, 16, R),
         vm(tiles, nz, 16, R), vm(tiles, nx, 16, R), vm(nx, 16, R), vm(tiles, nz, 16, R), vm(tiles, 16 * nz, R),
         vm(tiles, 2, 2 * V, 8, R), vm(tiles, 2, 2 * V, 8, R),
-        dma(11), dma(2), dma(2), dma(2, tiles), dma(2, tiles), pltpu.SemaphoreType.DMA, pltpu.SemaphoreType.DMA,
+        dma(15), dma(2, 2), dma(2, 2), dma(2, tiles), dma(2, tiles), pltpu.SemaphoreType.DMA, pltpu.SemaphoreType.DMA,
         dma(nz), dma(nz), dma(nx), dma(nx),
         dma(tiles), dma(tiles), dma(tiles, nz), dma(tiles, nz), dma(tiles, nx), dma(tiles, nx),
-        dma(tiles, nz), dma(tiles, nz), dma(tiles), dma(tiles), dma(tiles),
+        dma(tiles, nz), dma(tiles, nz), dma(tiles), dma(tiles), dma(tiles, 2),
     ]
-    return pl.pallas_call(
+    smem = pl.BlockSpec(memory_space=pltpu.SMEM)
+    out = pl.pallas_call(
         functools.partial(kernel, nx, nz, ny, cells, nt),
-        out_shape=jax.ShapeDtypeStruct(state.shape, F32),
-        in_specs=[ANY] * 11,
+        out_shape=jax.ShapeDtypeStruct((cells, V, nt, 2, R), F32),
+        in_specs=[ANY] * 6 + [smem] * 2 + [ANY] * 4,
         out_specs=ANY,
         scratch_shapes=scratch,
         compiler_params=pltpu.CompilerParams(collective_id=0, has_side_effects=True),
         name="line_update",
-    )(state, advect, viscous, inverse, lower, upper, row, *tables(nt))
+    )(
+        *(jnp.moveaxis(a, 1, -2) for a in (state, advect, viscous, inverse, lower, upper)),
+        blades, harmonic, *tables(nt),
+    )
+    return jnp.moveaxis(out, -2, 1)
 
 
 def solution(mesh):

time: 102 us -> 83.1 us (0.81)
  local copies, waits for them, and re-layouts: 21.5 us -> 4.37 us
  between operations: 1.36 us -> 0.01 us
    unnamed x6 -> x1, local copies, waits for them, and re-layouts: 13.2 us -> 4.37 us
    pallas_call x1 -> x0, local copies, waits for them, and re-layouts: 6.31 us -> none  [local(): pl.pallas_call(functools.partial(kernel, nx, nz, ny, cells, nt), out_shap...]
    slice x1 -> x0, local copies, waits for them, and re-layouts: 1.34 us -> none  [local(): ratio = blades[1].astype(F32) / blades[0].astype(F32)]
where the time goes in v2:
time: 83.1 us; the launch traced here: 83 us
  Pallas kernels  78.6 us (95%)
  local copies, waits for them, and re-layouts  4.37 us (5%)
    pallas_call x1, Pallas kernels, local(): pl.pallas_call(functools.partial(kernel, nx, nz, ny, cells, nt), out_shap...  78.6 us
    unnamed x1, local copies, waits for them, and re-layouts  4.37 us

profile of v2, /device:TPU:1, one launch (start us, length us, event | category | flops | bytes accessed | tf_op | source)
XLA Modules:
  0.0 83.0 jit_solution(6922004270775854374)
XLA Ops:
  0.0 78.6 %line_update.1 = f32[16,5,49,2,128]{4,3,2,1,0:T(2,128)} custom-call(f32[16,5,49,2,128]{4,3,2,1,0:T(2,128)} %bitcast.8, f32[16,5,2,128]{3,2,1,0:T(2,128)} %bitcast.12, f32[16,5,2,128]{3,2,1,0:T(2,128)} %bitcast.13, bf16[16,5,5,2,128]{4,3,2,1,0:T(2,128)(2,1)} %bitcast.11, f32[16,5,5,2,128]{4,3,2,1,0:T(2,128)} %bitcast.9, f32[16,5,5,2,128]{4,3,2,1,0:T(2,128)} %bitcast.10, ...), custom_call_target="tpu_custom_call" | custom-call | tf_op jit(solution)/shard_map/line_update/pallas_call | solution.py:670
  78.6 4.4 %copy.14 = f32[16,2,5,49,128]{4,1,3,2,0:T(2,128)} copy(f32[16,2,5,49,128]{4,1,3,2,0:T(2,128)} %bitcast.7) | data formatting | bytes 8028160
